TPU v7x, 32 devices: a whole 2x2x4 slice. The times are simulated.
32 devices in a mesh: section: 2 (over x), space: 16 (over z, y, core).
Axes of the slice: x: 2, y: 2, z: 4, core: 2. Of those that a mesh axis runs over, the one named last changes fastest.
Arguments:
- input_tiles: bfloat16 [16, 2, 4, 8, 8, 256], P('space'), may hold values from -6 to 6
- saved_tiles: bfloat16 [16, 2, 32, 4, 4, 128], P('space'), may hold values from -6 to 6
- out_grad_tiles: bfloat16 [16, 2, 64, 2, 2, 64], P('space'), may hold values from -1 to 1
- kernel_first: bfloat16 [32, 4, 3, 3, 3], replicated, may hold values from -0.625 to 0.625
- bias_first: float32 [32], replicated, may hold values from -3 to 3
- kernel_second: bfloat16 [64, 32, 3, 3, 3], replicated, may hold values from -0.21875 to 0.21875
- bias_second: float32 [64], replicated, may hold values from -3 to 3
Outputs:
- grad_kernel_first: float32 [32, 4, 3, 3, 3], replicated
- grad_bias_first: float32 [32], replicated
- grad_kernel_second: float32 [64, 32, 3, 3, 3], replicated
- grad_bias_second: float32 [64], replicated
All inputs are finite; a program needn't handle non-finite values.
Results may differ from a plain program's by a relative error of at most 0.0031.
Values may be sent and summed in bfloat16 or wider, within the bound.
No kernel may reach another device: no remote copies, remote signals or barrier semaphores. Data moves between devices by JAX's collectives and lax.ppermute only.
A program may use at most 128 MiB of HBM per device.

v0:
```python
import jax
import jax.numpy as jnp
from jax import lax
from jax.sharding import PartitionSpec as P

GY = 8


def from_behind(value, axis, steps):
    count = lax.axis_size(axis)
    first, last = (max(0, -steps), min(count, count - steps))
    return lax.ppermute(value, axis, [(source, source + steps) for source in range(first, last)])


def correlate(padded, kernel):
    return lax.conv_general_dilated(
        padded,
        kernel,
        (1, 1, 1),
        "VALID",
        dimension_numbers=("NCDHW", "OIDHW", "NCDHW"),
        preferred_element_type=jnp.float32,
    )


def kernel_grad(padded, grads):
    result = lax.conv_general_dilated(
        padded,
        grads,
        (1, 1, 1),
        "VALID",
        dimension_numbers=("CNDHW", "IODHW", "NCDHW"),
        preferred_element_type=jnp.float32,
    )
    return jnp.transpose(result, (1, 0, 2, 3, 4))


def flipped(kernel):
    return jnp.transpose(kernel[:, :, ::-1, ::-1, ::-1], (1, 0, 2, 3, 4))


def spread_up(grad):
    batch, channels, rows_y, rows_z, rows_x = grad.shape
    value = grad.astype(jnp.float32) * 0.125
    value = jnp.broadcast_to(
        value[:, :, :, None, :, None, :, None], (batch, channels, rows_y, 2, rows_z, 2, rows_x, 2)
    )
    return value.reshape(batch, channels, 2 * rows_y, 2 * rows_z, 2 * rows_x)


def slope(pre):
    return jnp.where(pre > 0, 1.0, 0.3)


def bias_column(bias):
    return bias[None, :, None, None, None]


def widen_last(field):
    return jnp.pad(field, ((0, 0), (0, 0), (0, 0), (0, 0), (1, 1)))


def extend(field):
    grid_z = lax.axis_size("space") // GY
    place = lax.axis_index("space") % grid_z
    last_plane = field[:, :, :, -1:]
    first_plane = field[:, :, :, :1]
    last_plane = jnp.where(place < grid_z - 1, last_plane, jnp.zeros_like(last_plane))
    first_plane = jnp.where(place > 0, first_plane, jnp.zeros_like(first_plane))
    low_z = from_behind(last_plane, "space", 1)
    high_z = from_behind(first_plane, "space", -1)
    wide = jnp.concatenate([low_z, field, high_z], axis=3)
    low_y = from_behind(wide[:, :, -1:], "space", grid_z)
    high_y = from_behind(wide[:, :, :1], "space", -grid_z)
    return widen_last(jnp.concatenate([low_y, wide, high_y], axis=2))


def second_delta(second_ext, cotangent, kernel_second, bias_second):
    pre_two = correlate(second_ext, kernel_second) + bias_column(bias_second)
    return (spread_up(cotangent) * slope(pre_two)).astype(jnp.bfloat16)


def first_grads(first_ext, arrived, kernel_first, bias_first):
    pre_one = correlate(first_ext, kernel_first) + bias_column(bias_first)
    delta_one = (spread_up(arrived) * slope(pre_one)).astype(jnp.bfloat16)
    return (
        kernel_grad(first_ext, delta_one),
        jnp.sum(delta_one, axis=(0, 2, 3, 4), dtype=jnp.float32),
    )


def on_device(
    input_tiles, saved_tiles, out_grad_tiles, kernel_first, bias_first, kernel_second, bias_second
):
    first = input_tiles[0]
    second = saved_tiles[0]
    cotangent = out_grad_tiles[0]
    section = lax.axis_index("section")
    batches = first.shape[0]
    flipped_two = flipped(kernel_second)
    share = batches // lax.axis_size("section")
    offset = section * share
    local_first = lax.dynamic_slice_in_dim(first, offset, share, 0)
    local_second = lax.dynamic_slice_in_dim(second, offset, share, 0)
    local_cot = lax.dynamic_slice_in_dim(cotangent, offset, share, 0)
    second_ext = extend(local_second)
    first_ext = extend(local_first)
    delta_two = second_delta(second_ext, local_cot, kernel_second, bias_second)
    delta_ext = extend(delta_two)
    grad_w_two = kernel_grad(second_ext, delta_two)
    grad_b_two = jnp.sum(delta_two, axis=(0, 2, 3, 4), dtype=jnp.float32)
    back = correlate(delta_ext, flipped_two).astype(jnp.bfloat16)
    grad_w_one, grad_b_one = first_grads(first_ext, back, kernel_first, bias_first)
    total = lax.psum((grad_w_one, grad_b_one, grad_w_two, grad_b_two), ("section", "space"))
    return (total[0], total[1], total[2], total[3])


def solution(mesh):
    placed = (
        P("space", None, None, None, None, None),
        P("space", None, None, None, None, None),
        P("space", None, None, None, None, None),
        P(),
        P(),
        P(),
        P(),
    )
    return jax.shard_map(
        on_device, mesh=mesh, in_specs=placed, out_specs=(P(), P(), P(), P()), check_vma=False
    )
```

profile of v0, /device:TPU:0, one launch (start us, length us, event | category | flops | bytes accessed | tf_op | source)
XLA Modules:
  0.0 405.5 jit_solution(2935043332899590350)
XLA Ops:
  8.2 2.4 collective-permute-start
  13.0 5.2 %collective-permute-start.4 = (bf16[1,32,4,1,128]{4,1,3,2,0:T(8,128)(2,1)S(1)}, bf16[1,32,4,1,128]{4,1,3,2,0:T(8,128)(2,1)S(1)}, u32[]{:S(2)}, u32[]{:S(2)}) collective-permute-start(bf16[1,32,4,1,128]{4,1,3,2,0:T(8,128)(2,1)S(1)} %get-tuple-element.19), channel_id=1, source_target_pairs={{0,1},{1,2},{2,3},{3,4},{4,5},{5,6},{6,7},{7,8},{8,9},{9,10},{10,1... | collective-permute-start | bytes 98312 | tf_op jit(solution)/shard_map/ppermute | solution.py:12
  20.3 9.1 %copy.94 = bf16[1,4,8,8,256]{1,0,4,3,2:T(2,128)(2,1)} copy(bf16[1,4,8,8,256]{4,3,2,1,0:T(8,128)(2,1)S(1)} %dynamic-slice_bitcast_fusion) | data formatting | bytes 262144 | tf_op jit(solution)/shard_map/dynamic_slice | solution.py:103
  30.8 7.0 %pad_maximum_fusion.3 = (bf16[1,4,1,10,256]{1,0,4,3,2:T(2,128)(2,1)}, bf16[1,4,1,10,256]{1,0,4,3,2:T(2,128)(2,1)}) fusion(bf16[1,4,8,1,256]{1,0,4,3,2:T(2,128)(2,1)S(1)} %copy.95, bf16[1,4,8,8,256]{1,0,4,3,2:T(2,128)(2,1)} %copy.94, bf16[1,4,8,1,256]{1,0,4,3,2:T(2,128)(2,1)S(1)} %copy.93), kind=kLoop, calls=%fused_computation.43 | loop fusion | flops 40960 | bytes 204800 | tf_op jit(solution)/shard_map/slice | solution.py:73
  37.9 2.5 copy.96
  40.4 5.9 %collective-permute-start.2 = (bf16[1,4,1,10,256]{4,1,3,2,0:T(4,128)(2,1)S(1)}, bf16[1,4,1,10,256]{4,1,3,2,0:T(4,128)(2,1)S(1)}, u32[]{:S(2)}, u32[]{:S(2)}) collective-permute-start(bf16[1,4,1,10,256]{4,1,3,2,0:T(4,128)(2,1)S(1)} %copy.96), channel_id=1, source_target_pairs={{0,2},{1,3},{2,4},{3,5},{4,6},{5,7},{6,8},{7,9},{8,10},{9,11},{10,... | collective-permute-start | bytes 61448 | tf_op jit(solution)/shard_map/ppermute | solution.py:12
  46.3 2.5 copy.97
  50.1 5.9 %collective-permute-start.6 = (bf16[1,32,1,6,128]{4,1,3,2,0:T(8,128)(2,1)S(1)}, bf16[1,32,1,6,128]{4,1,3,2,0:T(8,128)(2,1)S(1)}, u32[]{:S(2)}, u32[]{:S(2)}) collective-permute-start(bf16[1,32,1,6,128]{4,1,3,2,0:T(8,128)(2,1)S(1)} %get-tuple-element.17), channel_id=1, source_target_pairs={{0,2},{1,3},{2,4},{3,5},{4,6},{5,7},{6,8},{7,9},{8,10},{9,11},{10,... | collective-permute-start | bytes 147464 | tf_op jit(solution)/shard_map/ppermute | solution.py:12
  56.0 1.5 collective-permute-start.7
  57.5 2.2 copy.98
  59.7 2.2 copy.99
  61.8 40.1 %pad_maximum_fusion = bf16[1,4,10,10,256]{1,0,4,3,2:T(2,128)(2,1)} fusion(bf16[1,4,1,10,256]{1,0,4,3,2:T(2,128)(2,1)} %copy.99, bf16[1,4,8,1,256]{1,0,4,3,2:T(2,128)(2,1)S(1)} %copy.95, bf16[1,4,8,8,256]{1,0,4,3,2:T(2,128)(2,1)} %copy.94, bf16[1,4,8,1,256]{1,0,4,3,2:T(2,128)(2,1)S(1)} %copy.93, bf16[1,4,1,10,256]{1,0,4,3,2:T(2,128)(2,1)} %copy.98), kind=kLoop, calls=%fused_computation | loop fusion | flops 409600 | bytes 409600 | tf_op jit(solution)/shard_map/concatenate | solution.py:75
  101.9 23.7 %copy.113 = bf16[1,4,10,10,256]{4,1,3,2,0:T(4,128)(2,1)S(1)} copy(bf16[1,4,10,10,256]{1,0,4,3,2:T(2,128)(2,1)} %pad_maximum_fusion) | data formatting | bytes 409600 | tf_op jit(solution)/shard_map/concatenate | solution.py:75
  126.6 4.3 %copy.115 = bf16[4,10,10,1,8,33]{4,0,5,2,1,3:T(4,128)(2,1)} copy(bf16[4,10,10,1,8,33]{5,4,0,2,1,3:T(8,128)(2,1)S(1)} %reshape.57) | data formatting | bytes 422400 | tf_op jit(solution)/shard_map/conv_general_dilated | solution.py:16
  132.1 20.5 %fusion = f32[8,8,8,33,32]{4,2,3,1,0:T(8,128)S(1)} fusion(f32[32]{0:T(128)S(1)} %copy-done.9, pred[8,33]{0,1:T(8,128)(4,1)S(1)} %copy-done.11, bf16[32,4,3,3,3]{0,1,4,3,2:T(4,128)(2,1)S(1)} %copy-done.8, bf16[4,10,10,1,7,2]{4,0,5,2,1,3:T(4,128)(2,1)S(1)} %slice.64, bf16[4,10,10,1,8,33]{4,0,5,2,1,3:T(4,128)(2,1)} %copy.115), kind=kOutput, calls=%fused_computation.2 | convolution fusion | flops 119619840 | bytes 2392392 | tf_op jit(solution)/shard_map/conv_general_dilated | solution.py:16
  152.6 6.0 %copy.121 = f32[8,8,8,33,32]{4,3,2,1,0:T(8,128)} copy(f32[8,8,8,33,32]{4,2,3,1,0:T(8,128)S(1)} %fusion) | data formatting | bytes 4325376 | tf_op jit(solution)/shard_map/jit(_where)/select_n | solution.py:52
  158.6 9.5 %reshape.76 = f32[8,8,1,264,32]{4,3,1,0,2:T(8,128)} reshape(f32[8,8,8,33,32]{4,3,2,1,0:T(8,128)} %copy.121) | data formatting | bytes 4325376 | tf_op jit(solution)/shard_map/jit(_where)/select_n | solution.py:52
  169.0 1.7 reshape.45
  170.8 3.0 copy.103
  174.8 3.5 fusion.53
  180.0 1.4 broadcast_select_fusion.1
  181.6 2.0 collective-permute-start.8
  185.7 4.7 %copy.119 = bf16[1,32,6,6,128]{1,0,4,3,2:T(2,128)(2,1)S(1)} copy(bf16[1,32,6,6,128]{4,1,3,2,0:T(8,128)(2,1)} %pad_maximum_fusion.4) | data formatting | bytes 589824 | tf_op jit(solution)/shard_map/concatenate | solution.py:75
  193.2 7.7 %collective-permute-start.10 = (bf16[1,64,1,6,128]{4,1,3,2,0:T(8,128)(2,1)}, bf16[1,64,1,6,128]{4,1,3,2,0:T(8,128)(2,1)S(1)}, u32[]{:S(2)}, u32[]{:S(2)}) collective-permute-start(bf16[1,64,1,6,128]{4,1,3,2,0:T(8,128)(2,1)} %get-tuple-element.15), channel_id=1, source_target_pairs={{0,2},{1,3},{2,4},{3,5},{4,6},{5,7},{6,8},{7,9},{8,10},{9,11},{10,... | collective-permute-start | bytes 294920 | tf_op jit(solution)/shard_map/ppermute | solution.py:12
  201.0 1.5 collective-permute-start.11
  202.4 14.7 %fusion.58 = f32[64,32,3,3,3]{0,1,4,3,2:T(8,128)} fusion(bf16[1,32,6,6,128]{1,0,4,3,2:T(2,128)(2,1)S(1)} %copy.119, bf16[1,64,4,4,128]{1,3,4,2,0:T(4,128)(2,1)S(1)} %get-tuple-element.8), kind=kOutput, calls=%fused_computation.50 | convolution fusion | flops 225312768 | bytes 778240 | tf_op jit(solution)/shard_map/transpose | solution.py:35
  220.7 4.3 %fusion.50 = f32[4,4,8,17,32]{4,2,3,1,0:T(8,128)S(1)} fusion(bf16[64,32,3,3,3]{0,1,4,3,2:T(8,128)(2,1)S(1)} %copy-done.7, bf16[64,6,6,1,7,2]{0,4,5,2,1,3:T(8,128)(2,1)S(1)} %slice.62, bf16[64,6,6,1,8,17]{0,4,5,2,1,3:T(8,128)(2,1)S(1)} %copy.110, pred[8,17]{0,1:T(8,128)(4,1)S(1)} %copy-done.12), kind=kOutput, calls=%fused_computation.40 | convolution fusion | flops 243027968 | bytes 1080456 | tf_op jit(solution)/shard_map/conv_general_dilated | solution.py:16
  225.6 7.3 %broadcast_in_dim.41 = f32[32,4,2,4,2,128,2]{0,6,5,4,3,2,1:T(2,128)} broadcast(f32[32,4,4,128]{0,3,2,1:T(8,128)S(1)} %copy.112), dimensions={0,1,3,5} | broadcast | bytes 2359296 | tf_op jit(solution)/shard_map/broadcast_in_dim | solution.py:45
  232.9 7.6 %convert_reduce_fusion = (f32[32]{0:T(128)}, bf16[1,32,8,8,256]{1,4,3,2,0:T(8,128)(2,1)S(1)}) fusion(f32[1,32,8,8,256]{1,4,3,2,0:T(8,128)} %bitcast.76, f32[8,8,1,264,32]{4,3,1,0,2:T(8,128)} %reshape.76), kind=kLoop, calls=%fused_computation.6 | loop fusion | flops 2097120 | bytes 5243008 | tf_op jit(solution)/shard_map/reduce_sum | solution.py:88
  240.5 111.0 %fusion.3 = f32[32,4,3,3,3]{0,1,4,3,2:T(4,128)S(1)} fusion(bf16[1,4,10,10,256]{1,0,4,3,2:T(2,128)(2,1)} %pad_maximum_fusion, bf16[1,32,8,8,256]{1,4,3,2,0:T(8,128)(2,1)S(1)} %get-tuple-element.10), kind=kOutput, calls=%fused_computation.7 | convolution fusion | flops 112951296 | bytes 1267200 | tf_op jit(solution)/shard_map/transpose | solution.py:35
  351.5 44.9 %all-reduce = (f32[32,4,3,3,3]{0,1,4,3,2:T(4,128)}, f32[32]{0:T(128)}, f32[64]{0:T(128)}) all-reduce(f32[32,4,3,3,3]{0,1,4,3,2:T(4,128)S(1)} %fusion.3, f32[32]{0:T(128)S(1)} %copy-done.4, f32[64]{0:T(128)S(1)} %copy-done.5), channel_id=1, replica_groups=mesh['section'=2,'space'=16] {'section','space'}, use_global_device_ids=true, to_apply=%region_0.1 | all-reduce | flops 3552 | bytes 28416 | tf_op jit(solution)/shard_map/psum | solution.py:114
  396.4 1.8 copy.132
  (80 shorter events, 22.9 us)
Async XLA Ops:
  7.2 1.0 copy-start
  7.2 389.2 %all-reduce.3.cloned.1.call-start = ((), (), s32[]{:S(2)}) async-start(), calls=%async_computation | async-start | bytes 884736 | tf_op jit(solution)/shard_map/psum | solution.py:114
  8.2 21.3 %collective-permute-start = (bf16[1,4,8,1,256]{4,2,3,1,0:T(8,128)(2,1)S(1)}, bf16[1,4,8,1,256]{4,2,3,1,0:T(8,128)(2,1)S(1)}, u32[]{:S(2)}, u32[]{:S(2)}) collective-permute-start(bf16[1,4,8,1,256]{4,2,3,1,0:T(8,128)(2,1)S(1)} %copy.91), channel_id=1, source_target_pairs={{0,1},{1,2},{2,3},{3,4},{4,5},{5,6},{6,7},{7,8},{8,9},{9,10},{10,1... | collective-permute-start | bytes 49160 | tf_op jit(solution)/shard_map/ppermute | solution.py:12
  10.7 19.5 %collective-permute-start.1 = (bf16[1,4,8,1,256]{4,2,3,1,0:T(8,128)(2,1)S(1)}, bf16[1,4,8,1,256]{4,2,3,1,0:T(8,128)(2,1)S(1)}, u32[]{:S(2)}, u32[]{:S(2)}) collective-permute-start(bf16[1,4,8,1,256]{4,2,3,1,0:T(8,128)(2,1)S(1)} %copy.92), channel_id=1, source_target_pairs={{1,0},{2,1},{3,2},{4,3},{5,4},{6,5},{7,6},{8,7},{9,8},{10,9},{11,1... | collective-permute-start | bytes 49160 | tf_op jit(solution)/shard_map/ppermute | solution.py:12
  13.0 37.1 %collective-permute-start.4 = (bf16[1,32,4,1,128]{4,1,3,2,0:T(8,128)(2,1)S(1)}, bf16[1,32,4,1,128]{4,1,3,2,0:T(8,128)(2,1)S(1)}, u32[]{:S(2)}, u32[]{:S(2)}) collective-permute-start(bf16[1,32,4,1,128]{4,1,3,2,0:T(8,128)(2,1)S(1)} %get-tuple-element.19), channel_id=1, source_target_pairs={{0,1},{1,2},{2,3},{3,4},{4,5},{5,6},{6,7},{7,8},{8,9},{9,10},{10,1... | collective-permute-start | bytes 98312 | tf_op jit(solution)/shard_map/ppermute | solution.py:12
  18.1 32.0 %collective-permute-start.5 = (bf16[1,32,4,1,128]{4,1,3,2,0:T(8,128)(2,1)S(1)}, bf16[1,32,4,1,128]{4,1,3,2,0:T(8,128)(2,1)S(1)}, u32[]{:S(2)}, u32[]{:S(2)}) collective-permute-start(bf16[1,32,4,1,128]{4,1,3,2,0:T(8,128)(2,1)S(1)} %get-tuple-element.20), channel_id=1, source_target_pairs={{1,0},{2,1},{3,2},{4,3},{5,4},{6,5},{7,6},{8,7},{9,8},{10,9},{11,1... | collective-permute-start | bytes 98312 | tf_op jit(solution)/shard_map/ppermute | solution.py:12
  40.4 17.1 %collective-permute-start.2 = (bf16[1,4,1,10,256]{4,1,3,2,0:T(4,128)(2,1)S(1)}, bf16[1,4,1,10,256]{4,1,3,2,0:T(4,128)(2,1)S(1)}, u32[]{:S(2)}, u32[]{:S(2)}) collective-permute-start(bf16[1,4,1,10,256]{4,1,3,2,0:T(4,128)(2,1)S(1)} %copy.96), channel_id=1, source_target_pairs={{0,2},{1,3},{2,4},{3,5},{4,6},{5,7},{6,8},{7,9},{8,10},{9,11},{10,... | collective-permute-start | bytes 61448 | tf_op jit(solution)/shard_map/ppermute | solution.py:12
  48.8 10.9 %collective-permute-start.3 = (bf16[1,4,1,10,256]{4,1,3,2,0:T(4,128)(2,1)S(1)}, bf16[1,4,1,10,256]{4,1,3,2,0:T(4,128)(2,1)S(1)}, u32[]{:S(2)}, u32[]{:S(2)}) collective-permute-start(bf16[1,4,1,10,256]{4,1,3,2,0:T(4,128)(2,1)S(1)} %copy.97), channel_id=1, source_target_pairs={{2,0},{3,1},{4,2},{5,3},{6,4},{7,5},{8,6},{9,7},{10,8},{11,9},{12,... | collective-permute-start | bytes 61448 | tf_op jit(solution)/shard_map/ppermute | solution.py:12
  50.1 118.0 %collective-permute-start.6 = (bf16[1,32,1,6,128]{4,1,3,2,0:T(8,128)(2,1)S(1)}, bf16[1,32,1,6,128]{4,1,3,2,0:T(8,128)(2,1)S(1)}, u32[]{:S(2)}, u32[]{:S(2)}) collective-permute-start(bf16[1,32,1,6,128]{4,1,3,2,0:T(8,128)(2,1)S(1)} %get-tuple-element.17), channel_id=1, source_target_pairs={{0,2},{1,3},{2,4},{3,5},{4,6},{5,7},{6,8},{7,9},{8,10},{9,11},{10,... | collective-permute-start | bytes 147464 | tf_op jit(solution)/shard_map/ppermute | solution.py:12
  56.0 112.2 %collective-permute-start.7 = (bf16[1,32,1,6,128]{4,1,3,2,0:T(8,128)(2,1)S(1)}, bf16[1,32,1,6,128]{4,1,3,2,0:T(8,128)(2,1)S(1)}, u32[]{:S(2)}, u32[]{:S(2)}) collective-permute-start(bf16[1,32,1,6,128]{4,1,3,2,0:T(8,128)(2,1)S(1)} %get-tuple-element.18), channel_id=1, source_target_pairs={{2,0},{3,1},{4,2},{5,3},{6,4},{7,5},{8,6},{9,7},{10,8},{11,9},{12,... | collective-permute-start | bytes 147464 | tf_op jit(solution)/shard_map/ppermute | solution.py:12
  126.6 5.5 %copy-start.8 = (bf16[32,4,3,3,3]{0,1,4,3,2:T(4,128)(2,1)S(1)}, bf16[32,4,3,3,3]{0,1,4,3,2:T(4,128)(2,1)}, u32[]{:S(2)}) copy-start(bf16[32,4,3,3,3]{0,1,4,3,2:T(4,128)(2,1)} %param.10) | copy-start | bytes 20740
  126.6 5.5 %copy-start.9 = (f32[32]{0:T(128)S(1)}, f32[32]{0:T(128)}, u32[]{:S(2)}) copy-start(f32[32]{0:T(128)} %param.11) | copy-start | bytes 388
  126.6 5.5 %copy-start.11 = (pred[8,33]{0,1:T(8,128)(4,1)S(1)}, pred[8,33]{0,1:T(8,128)(4,1)}, u32[]{:S(2)}) copy-start(pred[8,33]{0,1:T(8,128)(4,1)} %constant.64) | copy-start | bytes 796
  168.2 0.6 copy-start.2
  170.8 4.0 copy-start.6
  170.8 4.0 copy-start.10
  170.8 4.0 copy-start.12
  178.9 6.1 %copy-start.3 = (bf16[1,32,1,6,128]{4,1,3,2,0:T(8,128)(2,1)S(1)}, bf16[1,32,1,6,128]{4,1,3,2,0:T(8,128)(2,1)}, u32[]{:S(2)}) copy-start(bf16[1,32,1,6,128]{4,1,3,2,0:T(8,128)(2,1)} %copy-done.2) | copy-start | bytes 147460
  181.6 8.8 %collective-permute-start.8 = (bf16[1,64,4,1,128]{1,3,4,2,0:T(2,128)(2,1)}, bf16[1,64,4,1,128]{1,3,4,2,0:T(2,128)(2,1)}, u32[]{:S(2)}, u32[]{:S(2)}) collective-permute-start(bf16[1,64,4,1,128]{1,3,4,2,0:T(2,128)(2,1)} %get-tuple-element.13), channel_id=1, source_target_pairs={{0,1},{1,2},{2,3},{3,4},{4,5},{5,6},{6,7},{7,8},{8,9},{9,10},{10,1... | collective-permute-start | bytes 196616 | tf_op jit(solution)/shard_map/ppermute | solution.py:12
  183.6 7.8 %collective-permute-start.9 = (bf16[1,64,4,1,128]{1,3,4,2,0:T(2,128)(2,1)}, bf16[1,64,4,1,128]{1,3,4,2,0:T(2,128)(2,1)}, u32[]{:S(2)}, u32[]{:S(2)}) collective-permute-start(bf16[1,64,4,1,128]{1,3,4,2,0:T(2,128)(2,1)} %get-tuple-element.14), channel_id=1, source_target_pairs={{1,0},{2,1},{3,2},{4,3},{5,4},{6,5},{7,6},{8,7},{9,8},{10,9},{11,1... | collective-permute-start | bytes 196616 | tf_op jit(solution)/shard_map/ppermute | solution.py:12
  193.2 24.0 %collective-permute-start.10 = (bf16[1,64,1,6,128]{4,1,3,2,0:T(8,128)(2,1)}, bf16[1,64,1,6,128]{4,1,3,2,0:T(8,128)(2,1)S(1)}, u32[]{:S(2)}, u32[]{:S(2)}) collective-permute-start(bf16[1,64,1,6,128]{4,1,3,2,0:T(8,128)(2,1)} %get-tuple-element.15), channel_id=1, source_target_pairs={{0,2},{1,3},{2,4},{3,5},{4,6},{5,7},{6,8},{7,9},{8,10},{9,11},{10,... | collective-permute-start | bytes 294920 | tf_op jit(solution)/shard_map/ppermute | solution.py:12
  201.0 16.2 %collective-permute-start.11 = (bf16[1,64,1,6,128]{4,1,3,2,0:T(8,128)(2,1)S(1)}, bf16[1,64,1,6,128]{4,1,3,2,0:T(8,128)(2,1)}, u32[]{:S(2)}, u32[]{:S(2)}) collective-permute-start(bf16[1,64,1,6,128]{4,1,3,2,0:T(8,128)(2,1)S(1)} %get-tuple-element.16), channel_id=1, source_target_pairs={{2,0},{3,1},{4,2},{5,3},{6,4},{7,5},{8,6},{9,7},{10,8},{11,9},{12,... | collective-permute-start | bytes 294920 | tf_op jit(solution)/shard_map/ppermute | solution.py:12
  219.8 0.9 copy-start.7
  240.5 111.0 %copy-start.4 = (f32[32]{0:T(128)S(1)}, f32[32]{0:T(128)}, u32[]{:S(2)}) copy-start(f32[32]{0:T(128)} %get-tuple-element.9) | copy-start | bytes 388
  240.5 111.0 %copy-start.5 = (f32[64]{0:T(128)S(1)}, f32[64]{0:T(128)}, u32[]{:S(2)}) copy-start(f32[64]{0:T(128)} %get-tuple-element.7) | copy-start | bytes 772
  240.5 157.7 %copy-start.1 = (bf16[1,2,4,8,8,256]{5,4,3,2,1,0:T(8,128)(2,1)S(1)}, bf16[1,2,4,8,8,256]{5,4,3,2,1,0:T(8,128)(2,1)}, u32[]{:S(2)}) copy-start(bf16[1,2,4,8,8,256]{5,4,3,2,1,0:T(8,128)(2,1)} %param.7) | copy-start | bytes 786436
Sparse Core Ops, SparseCore 0:
  217.3 131.7 all-reduce.2
where the time goes:
time: 411 us; the launch traced here: 406 us
  matrix products  154 us (37%)
  local copies, waits for them, and re-layouts  93.5 us (23%)
  other arithmetic  60.7 us (15%)
  blocking collectives  44.9 us (11%)
  starting transfers between devices  37.2 us (9%)
  between operations  15.1 us (4%)
    transpose x2, matrix products, kernel_grad(): return jnp.transpose(result, (1, 0, 2, 3, 4))  126 us
    psum x1, blocking collectives, on_device(): lax.psum((grad_w_one, grad_b_one, grad_w_two, grad_b_two), ('section', 's...  44.9 us
    concatenate x4, other arithmetic, extend(): return widen_last(jnp.concatenate([low_y, wide, high_y], axis=2))  41.9 us
    ppermute x12, starting transfers between devices, from_behind(): lax.ppermute(value, axis, [(source, source + steps) for source in range(f...  37.2 us
    concatenate x5, local copies, waits for them, and re-layouts, extend(): return widen_last(jnp.concatenate([low_y, wide, high_y], axis=2))  29.2 us
    conv_general_dilated x3, matrix products, correlate(): lax.conv_general_dilated(padded, kernel, (1, 1, 1), 'VALID', dimension_nu...  28.4 us
    select_n x3, local copies, waits for them, and re-layouts, slope(): return jnp.where(pre > 0, 1.0, 0.3)  15.8 us
    conv_general_dilated x9, local copies, waits for them, and re-layouts, correlate(): lax.conv_general_dilated(padded, kernel, (1, 1, 1), 'VALID', dimension_nu...  12.5 us
  transfers between devices with their start and end apart: 13, of which 0 were waited for; matrix products, arithmetic and copies ran while one was open for 71% of the time, Pallas kernels for 0%

commit v1 on v0

--- a/solution.py
+++ b/solution.py
@@ -111,7 +111,7 @@
     grad_b_two = jnp.sum(delta_two, axis=(0, 2, 3, 4), dtype=jnp.float32)
     back = correlate(delta_ext, flipped_two).astype(jnp.bfloat16)
     grad_w_one, grad_b_one = first_grads(first_ext, back, kernel_first, bias_first)
-    total = lax.psum((grad_w_one, grad_b_one, grad_w_two, grad_b_two), ("section", "space"))
+    total = lax.psum(lax.psum((grad_w_one, grad_b_one, grad_w_two, grad_b_two), "section"), "space")
     return (total[0], total[1], total[2], total[3])
 
 

time: 411 us -> 428 us (1.041)
  blocking collectives: 44.9 us -> 67.7 us
  matrix products: 154 us -> 140 us
  waiting for transfers between devices: 0.05 us -> 6.36 us
    psum x1 -> x2, blocking collectives: 44.9 us -> 67.7 us  [the longest x1 60.1 us: on_device(): lax.psum(lax.psum((grad_w_one, grad_b_one, grad_w_two, grad_b_two), 'sect...]
    transpose x2, matrix products: 126 us -> 112 us  [kernel_grad(): return jnp.transpose(result, (1, 0, 2, 3, 4))]
    psum x1 -> x2, waiting for transfers between devices: 0.01 us -> 6.3 us  [the longest x1 6.3 us: on_device(): lax.psum((grad_w_one, grad_b_one, grad_w_two, grad_b_two), 'section')]
  transfers between devices with their start and end apart: 13 -> 14, of which waited for: 0 -> 1; matrix products, arithmetic and copies ran while one was open for 71% -> 66% of each run, Pallas kernels for 0% -> 0%
where the time goes in v1:
time: 428 us; the launch traced here: 423 us
  matrix products  140 us (33%)
  local copies, waits for them, and re-layouts  93.6 us (22%)
  blocking collectives  67.7 us (16%)
  other arithmetic  62.7 us (15%)
  starting transfers between devices  37.2 us (9%)
  between operations  15.1 us (4%)
  waiting for transfers between devices  6.36 us (1%)
    transpose x2, matrix products, kernel_grad(): return jnp.transpose(result, (1, 0, 2, 3, 4))  112 us
    psum x1, blocking collectives, on_device(): lax.psum(lax.psum((grad_w_one, grad_b_one, grad_w_two, grad_b_two), 'sect...  60.1 us
    concatenate x4, other arithmetic, extend(): return widen_last(jnp.concatenate([low_y, wide, high_y], axis=2))  41.9 us
    ppermute x12, starting transfers between devices, from_behind(): lax.ppermute(value, axis, [(source, source + steps) for source in range(f...  37.2 us
    concatenate x5, local copies, waits for them, and re-layouts, extend(): return widen_last(jnp.concatenate([low_y, wide, high_y], axis=2))  29.2 us
    conv_general_dilated x3, matrix products, correlate(): lax.conv_general_dilated(padded, kernel, (1, 1, 1), 'VALID', dimension_nu...  28.3 us
    select_n x3, local copies, waits for them, and re-layouts, slope(): return jnp.where(pre > 0, 1.0, 0.3)  15.9 us
    conv_general_dilated x9, local copies, waits for them, and re-layouts, correlate(): lax.conv_general_dilated(padded, kernel, (1, 1, 1), 'VALID', dimension_nu...  12.5 us
  transfers between devices with their start and end apart: 14, of which 1 were waited for; matrix products, arithmetic and copies ran while one was open for 66% of the time, Pallas kernels for 0%

profile of v1, /device:TPU:0, one launch (start us, length us, event | category | flops | bytes accessed | tf_op | source)
XLA Modules:
  0.0 423.2 jit_solution(1498709366230446219)
XLA Ops:
  8.2 2.4 collective-permute-start
  13.0 5.2 %collective-permute-start.4 = (bf16[1,32,4,1,128]{4,1,3,2,0:T(8,128)(2,1)S(1)}, bf16[1,32,4,1,128]{4,1,3,2,0:T(8,128)(2,1)S(1)}, u32[]{:S(2)}, u32[]{:S(2)}) collective-permute-start(bf16[1,32,4,1,128]{4,1,3,2,0:T(8,128)(2,1)S(1)} %get-tuple-element.22), channel_id=1, source_target_pairs={{0,1},{1,2},{2,3},{3,4},{4,5},{5,6},{6,7},{7,8},{8,9},{9,10},{10,1... | collective-permute-start | bytes 98312 | tf_op jit(solution)/shard_map/ppermute | solution.py:12
  20.3 9.1 %copy.94 = bf16[1,4,8,8,256]{1,0,4,3,2:T(2,128)(2,1)} copy(bf16[1,4,8,8,256]{4,3,2,1,0:T(8,128)(2,1)S(1)} %dynamic-slice_bitcast_fusion) | data formatting | bytes 262144 | tf_op jit(solution)/shard_map/dynamic_slice | solution.py:103
  30.9 7.1 %pad_maximum_fusion.3 = (bf16[1,4,1,10,256]{1,0,4,3,2:T(2,128)(2,1)}, bf16[1,4,1,10,256]{1,0,4,3,2:T(2,128)(2,1)}) fusion(bf16[1,4,8,1,256]{1,0,4,3,2:T(2,128)(2,1)S(1)} %copy.95, bf16[1,4,8,8,256]{1,0,4,3,2:T(2,128)(2,1)} %copy.94, bf16[1,4,8,1,256]{1,0,4,3,2:T(2,128)(2,1)S(1)} %copy.93), kind=kLoop, calls=%fused_computation.43 | loop fusion | flops 40960 | bytes 204800 | tf_op jit(solution)/shard_map/slice | solution.py:73
  37.9 2.5 copy.96
  40.4 5.9 %collective-permute-start.2 = (bf16[1,4,1,10,256]{4,1,3,2,0:T(4,128)(2,1)S(1)}, bf16[1,4,1,10,256]{4,1,3,2,0:T(4,128)(2,1)S(1)}, u32[]{:S(2)}, u32[]{:S(2)}) collective-permute-start(bf16[1,4,1,10,256]{4,1,3,2,0:T(4,128)(2,1)S(1)} %copy.96), channel_id=1, source_target_pairs={{0,2},{1,3},{2,4},{3,5},{4,6},{5,7},{6,8},{7,9},{8,10},{9,11},{10,... | collective-permute-start | bytes 61448 | tf_op jit(solution)/shard_map/ppermute | solution.py:12
  46.3 2.5 copy.97
  50.2 5.9 %collective-permute-start.6 = (bf16[1,32,1,6,128]{4,1,3,2,0:T(8,128)(2,1)S(1)}, bf16[1,32,1,6,128]{4,1,3,2,0:T(8,128)(2,1)S(1)}, u32[]{:S(2)}, u32[]{:S(2)}) collective-permute-start(bf16[1,32,1,6,128]{4,1,3,2,0:T(8,128)(2,1)S(1)} %get-tuple-element.20), channel_id=1, source_target_pairs={{0,2},{1,3},{2,4},{3,5},{4,6},{5,7},{6,8},{7,9},{8,10},{9,11},{10,... | collective-permute-start | bytes 147464 | tf_op jit(solution)/shard_map/ppermute | solution.py:12
  56.0 1.5 collective-permute-start.7
  57.6 2.2 copy.98
  59.7 2.2 copy.99
  61.9 40.1 %pad_maximum_fusion = bf16[1,4,10,10,256]{1,0,4,3,2:T(2,128)(2,1)} fusion(bf16[1,4,1,10,256]{1,0,4,3,2:T(2,128)(2,1)} %copy.99, bf16[1,4,8,1,256]{1,0,4,3,2:T(2,128)(2,1)S(1)} %copy.95, bf16[1,4,8,8,256]{1,0,4,3,2:T(2,128)(2,1)} %copy.94, bf16[1,4,8,1,256]{1,0,4,3,2:T(2,128)(2,1)S(1)} %copy.93, bf16[1,4,1,10,256]{1,0,4,3,2:T(2,128)(2,1)} %copy.98), kind=kLoop, calls=%fused_computation | loop fusion | flops 409600 | bytes 409600 | tf_op jit(solution)/shard_map/concatenate | solution.py:75
  102.0 23.7 %copy.113 = bf16[1,4,10,10,256]{4,1,3,2,0:T(4,128)(2,1)S(1)} copy(bf16[1,4,10,10,256]{1,0,4,3,2:T(2,128)(2,1)} %pad_maximum_fusion) | data formatting | bytes 409600 | tf_op jit(solution)/shard_map/concatenate | solution.py:75
  126.7 4.3 %copy.115 = bf16[4,10,10,1,8,33]{4,0,5,2,1,3:T(4,128)(2,1)} copy(bf16[4,10,10,1,8,33]{5,4,0,2,1,3:T(8,128)(2,1)S(1)} %reshape.57) | data formatting | bytes 422400 | tf_op jit(solution)/shard_map/conv_general_dilated | solution.py:16
  132.1 20.5 %fusion = f32[8,8,8,33,32]{4,2,3,1,0:T(8,128)S(1)} fusion(f32[32]{0:T(128)S(1)} %copy-done.9, pred[8,33]{0,1:T(8,128)(4,1)S(1)} %copy-done.11, bf16[32,4,3,3,3]{0,1,4,3,2:T(4,128)(2,1)S(1)} %copy-done.8, bf16[4,10,10,1,7,2]{4,0,5,2,1,3:T(4,128)(2,1)S(1)} %slice.64, bf16[4,10,10,1,8,33]{4,0,5,2,1,3:T(4,128)(2,1)} %copy.115), kind=kOutput, calls=%fused_computation.2 | convolution fusion | flops 119619840 | bytes 2392392 | tf_op jit(solution)/shard_map/conv_general_dilated | solution.py:16
  152.7 6.0 %copy.121 = f32[8,8,8,33,32]{4,3,2,1,0:T(8,128)} copy(f32[8,8,8,33,32]{4,2,3,1,0:T(8,128)S(1)} %fusion) | data formatting | bytes 4325376 | tf_op jit(solution)/shard_map/jit(_where)/select_n | solution.py:52
  158.7 9.5 %reshape.76 = f32[8,8,1,264,32]{4,3,1,0,2:T(8,128)} reshape(f32[8,8,8,33,32]{4,3,2,1,0:T(8,128)} %copy.121) | data formatting | bytes 4325376 | tf_op jit(solution)/shard_map/jit(_where)/select_n | solution.py:52
  169.1 1.7 reshape.45
  170.9 3.0 copy.103
  174.9 3.5 fusion.53
  181.8 2.0 collective-permute-start.8
  185.8 4.7 %copy.119 = bf16[1,32,6,6,128]{1,0,4,3,2:T(2,128)(2,1)S(1)} copy(bf16[1,32,6,6,128]{4,1,3,2,0:T(8,128)(2,1)} %pad_maximum_fusion.4) | data formatting | bytes 589824 | tf_op jit(solution)/shard_map/concatenate | solution.py:75
  193.4 7.7 %collective-permute-start.10 = (bf16[1,64,1,6,128]{4,1,3,2,0:T(8,128)(2,1)}, bf16[1,64,1,6,128]{4,1,3,2,0:T(8,128)(2,1)S(1)}, u32[]{:S(2)}, u32[]{:S(2)}) collective-permute-start(bf16[1,64,1,6,128]{4,1,3,2,0:T(8,128)(2,1)} %get-tuple-element.18), channel_id=1, source_target_pairs={{0,2},{1,3},{2,4},{3,5},{4,6},{5,7},{6,8},{7,9},{8,10},{9,11},{10,... | collective-permute-start | bytes 294920 | tf_op jit(solution)/shard_map/ppermute | solution.py:12
  202.6 14.7 %fusion.58 = f32[64,32,3,3,3]{0,1,4,3,2:T(8,128)} fusion(bf16[1,32,6,6,128]{1,0,4,3,2:T(2,128)(2,1)S(1)} %copy.119, bf16[1,64,4,4,128]{1,3,4,2,0:T(4,128)(2,1)S(1)} %get-tuple-element.11), kind=kOutput, calls=%fused_computation.50 | convolution fusion | flops 225312768 | bytes 778240 | tf_op jit(solution)/shard_map/transpose | solution.py:35
  220.9 4.3 %fusion.50 = f32[4,4,8,17,32]{4,2,3,1,0:T(8,128)S(1)} fusion(bf16[64,32,3,3,3]{0,1,4,3,2:T(8,128)(2,1)S(1)} %copy-done.7, bf16[64,6,6,1,7,2]{0,4,5,2,1,3:T(8,128)(2,1)S(1)} %slice.62, bf16[64,6,6,1,8,17]{0,4,5,2,1,3:T(8,128)(2,1)S(1)} %copy.110, pred[8,17]{0,1:T(8,128)(4,1)S(1)} %copy-done.12), kind=kOutput, calls=%fused_computation.40 | convolution fusion | flops 243027968 | bytes 1080456 | tf_op jit(solution)/shard_map/conv_general_dilated | solution.py:16
  225.8 7.3 %broadcast_in_dim.41 = f32[32,4,2,4,2,128,2]{0,6,5,4,3,2,1:T(2,128)} broadcast(f32[32,4,4,128]{0,3,2,1:T(8,128)S(1)} %copy.112), dimensions={0,1,3,5} | broadcast | bytes 2359296 | tf_op jit(solution)/shard_map/broadcast_in_dim | solution.py:45
  233.1 9.6 %convert_reduce_fusion = (f32[32]{0:T(128)}, bf16[1,32,8,8,256]{1,4,3,2,0:T(8,128)(2,1)}) fusion(f32[1,32,8,8,256]{1,4,3,2,0:T(8,128)} %bitcast.76, f32[8,8,1,264,32]{4,3,1,0,2:T(8,128)} %reshape.76), kind=kLoop, calls=%fused_computation.6 | loop fusion | flops 2097120 | bytes 5243008 | tf_op jit(solution)/shard_map/reduce_sum | solution.py:88
  242.7 6.3 %all-reduce.5.cloned.1.call-done = f32[64,32,3,3,3]{0,1,4,3,2:T(8,128)} async-done(((f32[64,32,3,3,3]{0,1,4,3,2:T(8,128)}), f32[64,32,3,3,3]{0,1,4,3,2:T(8,128)}) %all-reduce.5.cloned.1.call-update) | async-done | bytes 221200 | tf_op jit(solution)/shard_map/psum | solution.py:114
  249.0 97.4 %fusion.3 = f32[32,4,3,3,3]{0,1,4,3,2:T(4,128)S(1)} fusion(bf16[1,4,10,10,256]{1,0,4,3,2:T(2,128)(2,1)} %pad_maximum_fusion, bf16[1,32,8,8,256]{1,4,3,2,0:T(8,128)(2,1)} %get-tuple-element.13), kind=kOutput, calls=%fused_computation.7 | convolution fusion | flops 112951296 | bytes 1267200 | tf_op jit(solution)/shard_map/transpose | solution.py:35
  346.4 7.6 %all-reduce.1 = (f32[32,4,3,3,3]{0,1,4,3,2:T(4,128)S(1)}, f32[32]{0:T(128)S(1)}, f32[64]{0:T(128)S(1)}) all-reduce(f32[32,4,3,3,3]{0,1,4,3,2:T(4,128)S(1)} %fusion.3, f32[32]{0:T(128)S(1)} %copy-done.4, f32[64]{0:T(128)S(1)} %copy-done.5), channel_id=1, replica_groups=mesh['section'=2,'space'=16] {'section'}, use_global_device_ids=true, to_apply=%region_0.1 | all-reduce | flops 3552 | bytes 28416 | tf_op jit(solution)/shard_map/psum | solution.py:114
  354.0 60.1 %all-reduce = (f32[32,4,3,3,3]{0,1,4,3,2:T(4,128)}, f32[32]{0:T(128)}, f32[64]{0:T(128)}) all-reduce(f32[32,4,3,3,3]{0,1,4,3,2:T(4,128)S(1)} %get-tuple-element.7, f32[32]{0:T(128)S(1)} %get-tuple-element.8, f32[64]{0:T(128)S(1)} %get-tuple-element.9), channel_id=1, replica_groups=mesh['section'=2,'space'=16] {'space'}, use_global_device_ids=true, to_apply=%region_1.2 | all-reduce | flops 3552 | bytes 28416 | tf_op jit(solution)/shard_map/psum | solution.py:114
  414.1 1.8 copy.133
  (84 shorter events, 25.8 us)
Async XLA Ops:
  7.2 1.0 copy-start
  7.2 241.8 %all-reduce.5.cloned.1.call-start = ((), (), s32[]{:S(2)}) async-start(), calls=%async_computation | async-start | bytes 884736 | tf_op jit(solution)/shard_map/psum | solution.py:114
  8.2 21.3 %collective-permute-start = (bf16[1,4,8,1,256]{4,2,3,1,0:T(8,128)(2,1)S(1)}, bf16[1,4,8,1,256]{4,2,3,1,0:T(8,128)(2,1)S(1)}, u32[]{:S(2)}, u32[]{:S(2)}) collective-permute-start(bf16[1,4,8,1,256]{4,2,3,1,0:T(8,128)(2,1)S(1)} %copy.91), channel_id=1, source_target_pairs={{0,1},{1,2},{2,3},{3,4},{4,5},{5,6},{6,7},{7,8},{8,9},{9,10},{10,1... | collective-permute-start | bytes 49160 | tf_op jit(solution)/shard_map/ppermute | solution.py:12
  10.7 19.6 %collective-permute-start.1 = (bf16[1,4,8,1,256]{4,2,3,1,0:T(8,128)(2,1)S(1)}, bf16[1,4,8,1,256]{4,2,3,1,0:T(8,128)(2,1)S(1)}, u32[]{:S(2)}, u32[]{:S(2)}) collective-permute-start(bf16[1,4,8,1,256]{4,2,3,1,0:T(8,128)(2,1)S(1)} %copy.92), channel_id=1, source_target_pairs={{1,0},{2,1},{3,2},{4,3},{5,4},{6,5},{7,6},{8,7},{9,8},{10,9},{11,1... | collective-permute-start | bytes 49160 | tf_op jit(solution)/shard_map/ppermute | solution.py:12
  13.0 37.2 %collective-permute-start.4 = (bf16[1,32,4,1,128]{4,1,3,2,0:T(8,128)(2,1)S(1)}, bf16[1,32,4,1,128]{4,1,3,2,0:T(8,128)(2,1)S(1)}, u32[]{:S(2)}, u32[]{:S(2)}) collective-permute-start(bf16[1,32,4,1,128]{4,1,3,2,0:T(8,128)(2,1)S(1)} %get-tuple-element.22), channel_id=1, source_target_pairs={{0,1},{1,2},{2,3},{3,4},{4,5},{5,6},{6,7},{7,8},{8,9},{9,10},{10,1... | collective-permute-start | bytes 98312 | tf_op jit(solution)/shard_map/ppermute | solution.py:12
  18.1 32.0 %collective-permute-start.5 = (bf16[1,32,4,1,128]{4,1,3,2,0:T(8,128)(2,1)S(1)}, bf16[1,32,4,1,128]{4,1,3,2,0:T(8,128)(2,1)S(1)}, u32[]{:S(2)}, u32[]{:S(2)}) collective-permute-start(bf16[1,32,4,1,128]{4,1,3,2,0:T(8,128)(2,1)S(1)} %get-tuple-element.23), channel_id=1, source_target_pairs={{1,0},{2,1},{3,2},{4,3},{5,4},{6,5},{7,6},{8,7},{9,8},{10,9},{11,1... | collective-permute-start | bytes 98312 | tf_op jit(solution)/shard_map/ppermute | solution.py:12
  40.4 17.1 %collective-permute-start.2 = (bf16[1,4,1,10,256]{4,1,3,2,0:T(4,128)(2,1)S(1)}, bf16[1,4,1,10,256]{4,1,3,2,0:T(4,128)(2,1)S(1)}, u32[]{:S(2)}, u32[]{:S(2)}) collective-permute-start(bf16[1,4,1,10,256]{4,1,3,2,0:T(4,128)(2,1)S(1)} %copy.96), channel_id=1, source_target_pairs={{0,2},{1,3},{2,4},{3,5},{4,6},{5,7},{6,8},{7,9},{8,10},{9,11},{10,... | collective-permute-start | bytes 61448 | tf_op jit(solution)/shard_map/ppermute | solution.py:12
  48.8 10.9 %collective-permute-start.3 = (bf16[1,4,1,10,256]{4,1,3,2,0:T(4,128)(2,1)S(1)}, bf16[1,4,1,10,256]{4,1,3,2,0:T(4,128)(2,1)S(1)}, u32[]{:S(2)}, u32[]{:S(2)}) collective-permute-start(bf16[1,4,1,10,256]{4,1,3,2,0:T(4,128)(2,1)S(1)} %copy.97), channel_id=1, source_target_pairs={{2,0},{3,1},{4,2},{5,3},{6,4},{7,5},{8,6},{9,7},{10,8},{11,9},{12,... | collective-permute-start | bytes 61448 | tf_op jit(solution)/shard_map/ppermute | solution.py:12
  50.2 118.0 %collective-permute-start.6 = (bf16[1,32,1,6,128]{4,1,3,2,0:T(8,128)(2,1)S(1)}, bf16[1,32,1,6,128]{4,1,3,2,0:T(8,128)(2,1)S(1)}, u32[]{:S(2)}, u32[]{:S(2)}) collective-permute-start(bf16[1,32,1,6,128]{4,1,3,2,0:T(8,128)(2,1)S(1)} %get-tuple-element.20), channel_id=1, source_target_pairs={{0,2},{1,3},{2,4},{3,5},{4,6},{5,7},{6,8},{7,9},{8,10},{9,11},{10,... | collective-permute-start | bytes 147464 | tf_op jit(solution)/shard_map/ppermute | solution.py:12
  56.0 112.2 %collective-permute-start.7 = (bf16[1,32,1,6,128]{4,1,3,2,0:T(8,128)(2,1)S(1)}, bf16[1,32,1,6,128]{4,1,3,2,0:T(8,128)(2,1)S(1)}, u32[]{:S(2)}, u32[]{:S(2)}) collective-permute-start(bf16[1,32,1,6,128]{4,1,3,2,0:T(8,128)(2,1)S(1)} %get-tuple-element.21), channel_id=1, source_target_pairs={{2,0},{3,1},{4,2},{5,3},{6,4},{7,5},{8,6},{9,7},{10,8},{11,9},{12,... | collective-permute-start | bytes 147464 | tf_op jit(solution)/shard_map/ppermute | solution.py:12
  126.6 5.4 %copy-start.8 = (bf16[32,4,3,3,3]{0,1,4,3,2:T(4,128)(2,1)S(1)}, bf16[32,4,3,3,3]{0,1,4,3,2:T(4,128)(2,1)}, u32[]{:S(2)}) copy-start(bf16[32,4,3,3,3]{0,1,4,3,2:T(4,128)(2,1)} %param.10) | copy-start | bytes 20740
  126.7 5.4 %copy-start.9 = (f32[32]{0:T(128)S(1)}, f32[32]{0:T(128)}, u32[]{:S(2)}) copy-start(f32[32]{0:T(128)} %param.11) | copy-start | bytes 388
  126.7 5.4 %copy-start.11 = (pred[8,33]{0,1:T(8,128)(4,1)S(1)}, pred[8,33]{0,1:T(8,128)(4,1)}, u32[]{:S(2)}) copy-start(pred[8,33]{0,1:T(8,128)(4,1)} %constant.64) | copy-start | bytes 796
  168.2 0.6 copy-start.2
  170.8 4.0 copy-start.6
  170.8 4.0 copy-start.10
  170.9 4.0 copy-start.12
  179.0 6.1 %copy-start.3 = (bf16[1,32,1,6,128]{4,1,3,2,0:T(8,128)(2,1)S(1)}, bf16[1,32,1,6,128]{4,1,3,2,0:T(8,128)(2,1)}, u32[]{:S(2)}) copy-start(bf16[1,32,1,6,128]{4,1,3,2,0:T(8,128)(2,1)} %copy-done.2) | copy-start | bytes 147460
  181.8 8.8 %collective-permute-start.8 = (bf16[1,64,4,1,128]{1,3,4,2,0:T(2,128)(2,1)}, bf16[1,64,4,1,128]{1,3,4,2,0:T(2,128)(2,1)}, u32[]{:S(2)}, u32[]{:S(2)}) collective-permute-start(bf16[1,64,4,1,128]{1,3,4,2,0:T(2,128)(2,1)} %get-tuple-element.16), channel_id=1, source_target_pairs={{0,1},{1,2},{2,3},{3,4},{4,5},{5,6},{6,7},{7,8},{8,9},{9,10},{10,1... | collective-permute-start | bytes 196616 | tf_op jit(solution)/shard_map/ppermute | solution.py:12
  183.8 7.8 %collective-permute-start.9 = (bf16[1,64,4,1,128]{1,3,4,2,0:T(2,128)(2,1)}, bf16[1,64,4,1,128]{1,3,4,2,0:T(2,128)(2,1)}, u32[]{:S(2)}, u32[]{:S(2)}) collective-permute-start(bf16[1,64,4,1,128]{1,3,4,2,0:T(2,128)(2,1)} %get-tuple-element.17), channel_id=1, source_target_pairs={{1,0},{2,1},{3,2},{4,3},{5,4},{6,5},{7,6},{8,7},{9,8},{10,9},{11,1... | collective-permute-start | bytes 196616 | tf_op jit(solution)/shard_map/ppermute | solution.py:12
  193.4 24.0 %collective-permute-start.10 = (bf16[1,64,1,6,128]{4,1,3,2,0:T(8,128)(2,1)}, bf16[1,64,1,6,128]{4,1,3,2,0:T(8,128)(2,1)S(1)}, u32[]{:S(2)}, u32[]{:S(2)}) collective-permute-start(bf16[1,64,1,6,128]{4,1,3,2,0:T(8,128)(2,1)} %get-tuple-element.18), channel_id=1, source_target_pairs={{0,2},{1,3},{2,4},{3,5},{4,6},{5,7},{6,8},{7,9},{8,10},{9,11},{10,... | collective-permute-start | bytes 294920 | tf_op jit(solution)/shard_map/ppermute | solution.py:12
  201.1 16.3 %collective-permute-start.11 = (bf16[1,64,1,6,128]{4,1,3,2,0:T(8,128)(2,1)S(1)}, bf16[1,64,1,6,128]{4,1,3,2,0:T(8,128)(2,1)}, u32[]{:S(2)}, u32[]{:S(2)}) collective-permute-start(bf16[1,64,1,6,128]{4,1,3,2,0:T(8,128)(2,1)S(1)} %get-tuple-element.19), channel_id=1, source_target_pairs={{2,0},{3,1},{4,2},{5,3},{6,4},{7,5},{8,6},{9,7},{10,8},{11,9},{12,... | collective-permute-start | bytes 294920 | tf_op jit(solution)/shard_map/ppermute | solution.py:12
  217.3 196.8 %all-reduce.7.cloned.1.call-start = ((), (), s32[]{:S(2)}) async-start(), calls=%async_computation.1 | async-start | bytes 884736 | tf_op jit(solution)/shard_map/psum | solution.py:114
  220.0 0.9 copy-start.7
  249.0 97.4 %copy-start.4 = (f32[32]{0:T(128)S(1)}, f32[32]{0:T(128)}, u32[]{:S(2)}) copy-start(f32[32]{0:T(128)} %get-tuple-element.12) | copy-start | bytes 388
  249.0 97.4 %copy-start.5 = (f32[64]{0:T(128)S(1)}, f32[64]{0:T(128)}, u32[]{:S(2)}) copy-start(f32[64]{0:T(128)} %get-tuple-element.10) | copy-start | bytes 772
  249.0 166.9 %copy-start.1 = (bf16[1,2,4,8,8,256]{5,4,3,2,1,0:T(8,128)(2,1)S(1)}, bf16[1,2,4,8,8,256]{5,4,3,2,1,0:T(8,128)(2,1)}, u32[]{:S(2)}) copy-start(bf16[1,2,4,8,8,256]{5,4,3,2,1,0:T(8,128)(2,1)} %param.7) | copy-start | bytes 786436
Sparse Core Ops, SparseCore 0:
  217.4 31.4 all-reduce.4
  252.4 90.4 all-reduce.6
